TPU v7x, 32 devices: a whole 2x2x4 slice. The times are simulated.
32 devices in a mesh: rows: 8 (over y, x, core), snaps: 4 (over z).
Axes of the slice: x: 2, y: 2, z: 4, core: 2. Of those that a mesh axis runs over, the one named last changes fastest.
Arguments:
- snapshots: float32 [2048, 3072], P('rows', 'snaps'), may hold values from -6 to 6
Outputs:
- updated: float32 [2048, 3072], P('rows', 'snaps')
- factor_rows: float32 [1152, 3072], P(None, 'snaps')
All inputs are finite; a program needn't handle non-finite values.
Results may differ from a plain program's by a relative error of at most 0.00013.
Values sent between devices are 32-bit elements; how exact they have to be, the bound alone decides.
A program may use at most 64 MiB of HBM per device.

v0:
```python
import jax
import jax.numpy as jnp
from jax import lax
from jax.sharding import PartitionSpec as P

PANEL = 384
PANELS = 3


def spread(shard, axis, root):
    mine = lax.axis_index(axis) == root
    return lax.psum(jnp.where(mine, shard, jnp.zeros_like(shard)), axis)


def mult(left, right):
    return jnp.dot(left, right, precision=lax.Precision.HIGHEST, preferred_element_type=jnp.float32)


def fetch_panel(section, column_piece, n_snaps):
    return spread(column_piece, "snaps", section % n_snaps)


def shards(snapshots):
    rows_dev, cols_dev = snapshots.shape
    panel_width = PANEL
    n_snaps = lax.axis_size("snaps")
    my_snap = lax.axis_index("snaps")
    local_blocks = cols_dev // panel_width
    row_count = rows_dev * lax.axis_size("rows")
    root_rows = jnp.sqrt(jnp.float32(row_count))
    col_ids = jnp.arange(cols_dev, dtype=jnp.int32)
    turn_cols = col_ids // panel_width * n_snaps + my_snap
    identity = jnp.eye(panel_width, dtype=jnp.float32)
    working = snapshots
    coeff_rows = []
    slot_first = 0
    pending = fetch_panel(0, working[:, slot_first : slot_first + panel_width], n_snaps)
    for section in range(PANELS):
        panel_now = pending
        slot_index = section // n_snaps
        gram_matrix, cross_sums = lax.psum(
            (mult(panel_now.T, panel_now), mult(panel_now.T, working)), "rows"
        )
        factor = jnp.linalg.cholesky(gram_matrix)
        inverse = lax.linalg.triangular_solve(factor, identity, left_side=True, lower=True)
        orthobasis = mult(panel_now, inverse.T)
        coeffs = mult(inverse, cross_sums)
        applied = jnp.where((turn_cols > section)[None, :], coeffs, jnp.float32(0.0))
        working = working - mult(orthobasis, applied)
        low_own = slot_index * panel_width
        is_owner = my_snap == section % n_snaps
        own_cols = jnp.where(
            is_owner, orthobasis * root_rows, working[:, low_own : low_own + panel_width]
        )
        working = working.at[:, low_own : low_own + panel_width].set(own_cols)
        if section + 1 < PANELS:
            next_slot = (section + 1) // n_snaps
            low = next_slot * panel_width
            pending = fetch_panel(section + 1, working[:, low : low + panel_width], n_snaps)
        diagonal = jnp.where(
            (turn_cols == section)[None, :], jnp.tile(factor.T, (1, local_blocks)), jnp.float32(0.0)
        )
        coeff_rows.append((applied + diagonal) / root_rows)
    return (working, jnp.concatenate(coeff_rows, axis=0))


def solution(mesh):
    placed = (P("rows", "snaps"),)
    return jax.shard_map(
        shards,
        mesh=mesh,
        in_specs=placed,
        out_specs=(P("rows", "snaps"), P(None, "snaps")),
        check_vma=False,
    )
```

profile of v0, /device:TPU:0, one launch (start us, length us, event | category | flops | bytes accessed | tf_op | source)
XLA Modules:
  0.0 696.9 jit_solution(14924972085822224887)
XLA Ops:
  7.2 1.8 slice_select_fusion
  9.1 41.5 %all-reduce.11.cloned.1.call-done = f32[256,384]{1,0:T(8,128)} async-done(((f32[256,384]{1,0:T(8,128)}), f32[256,384]{1,0:T(8,128)}) %all-reduce.11.cloned.1.call-update) | async-done | bytes 393232 | tf_op jit(solution)/shard_map/psum | solution.py:12
  50.6 2.8 fusion.82
  53.4 2.1 fusion.83
  56.5 58.8 %all-reduce.21.cloned.1.call-done = (f32[384,384]{0,1:T(8,128)}, f32[384,768]{1,0:T(8,128)}) async-done(((f32[384,384]{0,1:T(8,128)}, f32[384,768]{1,0:T(8,128)}), (f32[384,384]{0,1:T(8,128)}, f32[384,768]{1,0:T(8,128)})) %all-reduce.21.cloned.1.call-update) | async-done | bytes 1769488 | tf_op jit(solution)/shard_map/psum | solution.py:41
  115.3 1.4 copy.4
  116.8 11.7 %cholesky.273 = f32[128,128]{1,0:T(8,128)S(1)} custom-call(f32[128,128]{1,0:T(8,128)S(1)} %cholesky.428), custom_call_target="Cholesky" | custom-call | tf_op jit(solution)/shard_map/jit(cholesky)/cholesky | solution.py:44
  128.6 9.8 %custom-call.23 = f32[1,128,128]{1,2,0:T(8,128)S(1)} custom-call(f32[1,128,128]{2,1,0:T(8,128)S(1)} %get-tuple-element.129), custom_call_target="InvertDiagBlocksLowerTriangular" | custom-call | tf_op jit(solution)/shard_map/jit(cholesky)/cholesky | solution.py:44
  139.0 11.7 %cholesky.292 = f32[128,128]{1,0:T(8,128)S(1)} custom-call(f32[128,128]{1,0:T(8,128)S(1)} %cholesky.432), custom_call_target="Cholesky" | custom-call | tf_op jit(solution)/shard_map/jit(cholesky)/cholesky | solution.py:44
  150.7 10.0 %custom-call.24 = f32[1,128,128]{1,2,0:T(8,128)S(1)} custom-call(f32[1,128,128]{2,1,0:T(8,128)S(1)} %get-tuple-element.126), custom_call_target="InvertDiagBlocksLowerTriangular" | custom-call | tf_op jit(solution)/shard_map/jit(cholesky)/cholesky | solution.py:44
  161.2 11.7 %cholesky.311 = f32[128,128]{1,0:T(8,128)S(1)} custom-call(f32[128,128]{1,0:T(8,128)S(1)} %convolution_subtract_fusion.14), custom_call_target="Cholesky" | custom-call | tf_op jit(solution)/shard_map/jit(cholesky)/cholesky | solution.py:44
  176.4 6.0 while.9
  177.0 1.4 bitcast_dynamic-update-slice_fusion.6
  179.0 1.4 bitcast_dynamic-update-slice_fusion.6
  181.0 1.4 bitcast_dynamic-update-slice_fusion.6
  183.2 29.9 %custom-call.25 = f32[3,128,128]{1,2,0:T(8,128)S(1)} custom-call(f32[3,128,128]{2,1,0:T(8,128)S(1)} %get-tuple-element.60), custom_call_target="InvertDiagBlocksLowerTriangular" | custom-call | tf_op jit(solution)/shard_map/triangular_solve/custom-call.2 | solution.py:45
  215.0 1.3 convolution_subtract_fusion.7
  218.6 2.1 add_multiply_fusion.2
  221.6 1.4 convolution_subtract_fusion.2
  223.1 1.4 broadcast_select_fusion.1
  224.6 36.4 %all-reduce.13.cloned.1.call-done = f32[256,384]{1,0:T(8,128)} async-done(((f32[256,384]{1,0:T(8,128)}), f32[256,384]{1,0:T(8,128)}) %all-reduce.13.cloned.1.call-update) | async-done | bytes 393232 | tf_op jit(solution)/shard_map/psum | solution.py:12
  261.0 2.8 fusion.84
  263.8 2.1 fusion.85
  266.2 59.5 %all-reduce.19.cloned.1.call-done = (f32[384,384]{0,1:T(8,128)}, f32[384,768]{1,0:T(8,128)}) async-done(((f32[384,384]{0,1:T(8,128)}, f32[384,768]{1,0:T(8,128)}), (f32[384,384]{0,1:T(8,128)}, f32[384,768]{1,0:T(8,128)})) %all-reduce.19.cloned.1.call-update) | async-done | bytes 1769488 | tf_op jit(solution)/shard_map/psum | solution.py:41
  325.7 2.1 copy.6
  327.8 1.3 fusion.1
  330.0 11.7 %cholesky.326 = f32[128,128]{1,0:T(8,128)S(1)} custom-call(f32[128,128]{1,0:T(8,128)S(1)} %cholesky.436), custom_call_target="Cholesky" | custom-call | tf_op jit(solution)/shard_map/jit(cholesky)/cholesky | solution.py:44
  342.6 9.8 %custom-call.26 = f32[1,128,128]{1,2,0:T(8,128)S(1)} custom-call(f32[1,128,128]{2,1,0:T(8,128)S(1)} %get-tuple-element.122), custom_call_target="InvertDiagBlocksLowerTriangular" | custom-call | tf_op jit(solution)/shard_map/jit(cholesky)/cholesky | solution.py:44
  352.4 1.8 constant_dynamic-update-slice_fusion.3
  355.4 11.7 %cholesky.345 = f32[128,128]{1,0:T(8,128)S(1)} custom-call(f32[128,128]{1,0:T(8,128)S(1)} %cholesky.440), custom_call_target="Cholesky" | custom-call | tf_op jit(solution)/shard_map/jit(cholesky)/cholesky | solution.py:44
  367.7 10.2 %custom-call.27 = f32[1,128,128]{1,2,0:T(8,128)S(1)} custom-call(f32[1,128,128]{2,1,0:T(8,128)S(1)} %get-tuple-element.119), custom_call_target="InvertDiagBlocksLowerTriangular" | custom-call | tf_op jit(solution)/shard_map/jit(cholesky)/cholesky | solution.py:44
  380.0 11.7 %cholesky.364 = f32[128,128]{1,0:T(8,128)S(1)} custom-call(f32[128,128]{1,0:T(8,128)S(1)} %convolution_subtract_fusion.13), custom_call_target="Cholesky" | custom-call | tf_op jit(solution)/shard_map/jit(cholesky)/cholesky | solution.py:44
  396.3 2.2 fusion.9
  398.4 8.7 %while.10 = (s32[]{:T(128)}, f32[384,384]{1,0:T(8,128)}, s32[3,2]{0,1:T(2,128)S(1)}, f32[3,128,128]{2,1,0:T(8,128)S(1)}, s32[]{:T(128)}) while((s32[]{:T(128)}, f32[384,384]{1,0:T(8,128)}, s32[3,2]{0,1:T(2,128)S(1)}, f32[3,128,128]{2,1,0:T(8,128)S(1)}, s32[]{:T(128)}) %tuple.117), condition=%wide.while_cond.3.clone, body=%wide.while_body.3.clone.sunk | while | flops 2 | bytes 131189 | solution.py:45
  399.1 2.2 bitcast_dynamic-update-slice_fusion.7
  402.0 2.2 bitcast_dynamic-update-slice_fusion.7
  404.9 2.2 bitcast_dynamic-update-slice_fusion.7
  407.1 29.5 %custom-call.28 = f32[3,128,128]{1,2,0:T(8,128)S(1)} custom-call(f32[3,128,128]{2,1,0:T(8,128)S(1)} %get-tuple-element.61), custom_call_target="InvertDiagBlocksLowerTriangular" | custom-call | tf_op jit(solution)/shard_map/triangular_solve/custom-call.2 | solution.py:45
  441.1 2.1 copy.10
  443.2 1.5 tile.14
  445.9 3.1 add_multiply_fusion.1
  450.0 1.4 convolution_subtract_fusion.1
  451.5 1.4 broadcast_select_fusion
  453.1 36.2 %all-reduce.15.cloned.1.call-done = f32[256,384]{1,0:T(8,128)} async-done(((f32[256,384]{1,0:T(8,128)}), f32[256,384]{1,0:T(8,128)}) %all-reduce.15.cloned.1.call-update) | async-done | bytes 393232 | tf_op jit(solution)/shard_map/psum | solution.py:12
  489.3 2.8 fusion.86
  492.1 2.2 fusion.87
  494.4 59.7 %all-reduce.17.cloned.1.call-done = (f32[384,384]{0,1:T(8,128)}, f32[384,768]{1,0:T(8,128)}) async-done(((f32[384,384]{0,1:T(8,128)}, f32[384,768]{1,0:T(8,128)}), (f32[384,384]{0,1:T(8,128)}, f32[384,768]{1,0:T(8,128)})) %all-reduce.17.cloned.1.call-update) | async-done | bytes 1769488 | tf_op jit(solution)/shard_map/psum | solution.py:41
  554.1 2.2 copy.8
  558.2 11.7 %cholesky.379 = f32[128,128]{1,0:T(8,128)S(1)} custom-call(f32[128,128]{1,0:T(8,128)S(1)} %cholesky.444), custom_call_target="Cholesky" | custom-call | tf_op jit(solution)/shard_map/jit(cholesky)/cholesky | solution.py:44
  572.1 11.3 %custom-call.29 = f32[1,128,128]{1,2,0:T(8,128)} custom-call(f32[1,128,128]{2,1,0:T(8,128)} %get-tuple-element.115), custom_call_target="InvertDiagBlocksLowerTriangular" | custom-call | tf_op jit(solution)/shard_map/jit(cholesky)/cholesky | solution.py:44
  587.0 13.3 %cholesky.398 = f32[128,128]{1,0:T(8,128)} custom-call(f32[128,128]{1,0:T(8,128)} %cholesky.448), custom_call_target="Cholesky" | custom-call | tf_op jit(solution)/shard_map/jit(cholesky)/cholesky | solution.py:44
  600.3 2.0 select_reduce_fusion.1
  602.3 11.3 %custom-call.30 = f32[1,128,128]{1,2,0:T(8,128)} custom-call(f32[1,128,128]{2,1,0:T(8,128)} %get-tuple-element.112), custom_call_target="InvertDiagBlocksLowerTriangular" | custom-call | tf_op jit(solution)/shard_map/jit(cholesky)/cholesky | solution.py:44
  614.7 1.7 convolution_subtract_fusion.12
  616.4 13.2 %cholesky.417 = f32[128,128]{1,0:T(8,128)} custom-call(f32[128,128]{1,0:T(8,128)} %convolution_subtract_fusion.12), custom_call_target="Cholesky" | custom-call | tf_op jit(solution)/shard_map/jit(cholesky)/cholesky | solution.py:44
  631.1 1.3 compare_reduce_fusion.1
  636.1 8.8 %while.11 = (s32[]{:T(128)}, f32[384,384]{1,0:T(8,128)}, s32[3,2]{0,1:T(2,128)S(1)}, f32[3,128,128]{2,1,0:T(8,128)S(1)}, s32[]{:T(128)}) while((s32[]{:T(128)}, f32[384,384]{1,0:T(8,128)}, s32[3,2]{0,1:T(2,128)S(1)}, f32[3,128,128]{2,1,0:T(8,128)S(1)}, s32[]{:T(128)}) %tuple.118), condition=%wide.while_cond.3.clone.1, body=%wide.while_body.3.clone.1.sunk | while | flops 2 | bytes 131189 | solution.py:45
  637.0 2.2 bitcast_dynamic-update-slice_fusion.8
  639.9 2.2 bitcast_dynamic-update-slice_fusion.8
  642.8 2.2 bitcast_dynamic-update-slice_fusion.8
  645.0 29.5 %custom-call.31 = f32[3,128,128]{1,2,0:T(8,128)S(1)} custom-call(f32[3,128,128]{2,1,0:T(8,128)S(1)} %get-tuple-element.62), custom_call_target="InvertDiagBlocksLowerTriangular" | custom-call | tf_op jit(solution)/shard_map/triangular_solve/custom-call.2 | solution.py:45
  681.9 2.1 add_multiply_fusion
  685.0 1.5 convolution_subtract_fusion
  687.7 2.0 pad_maximum_fusion
  (139 shorter events, 52.2 us)
Async XLA Ops:
  7.2 43.5 %all-reduce.11.cloned.1.call-start = ((), (), s32[]{:S(2)}) async-start(), calls=%async_computation | async-start | bytes 786432 | tf_op jit(solution)/shard_map/psum | solution.py:12
  7.2 46.2 %copy-start.3 = (f32[256,768]{1,0:T(8,128)S(1)}, f32[256,768]{1,0:T(8,128)}, u32[]{:S(2)}) copy-start(f32[256,768]{1,0:T(8,128)} %param.10) | copy-start | bytes 2359300
  9.1 106.2 %all-reduce.21.cloned.1.call-start = ((), (), s32[]{:S(2)}) async-start(), calls=%async_computation.5 | async-start | bytes 3538944 | tf_op jit(solution)/shard_map/psum | solution.py:41
  50.6 2.8 copy-start
  55.6 205.4 %all-reduce.13.cloned.1.call-start = ((), (), s32[]{:S(2)}) async-start(), calls=%async_computation.1 | async-start | bytes 786432 | tf_op jit(solution)/shard_map/psum | solution.py:12
  115.3 1.4 copy-start.5
  182.4 0.8 copy-start.7
  217.3 1.3 copy-start.11
  224.6 101.1 %all-reduce.19.cloned.1.call-start = ((), (), s32[]{:S(2)}) async-start(), calls=%async_computation.4 | async-start | bytes 3538944 | tf_op jit(solution)/shard_map/psum | solution.py:41
  261.0 2.8 copy-start.1
  266.0 223.4 %all-reduce.15.cloned.1.call-start = ((), (), s32[]{:S(2)}) async-start(), calls=%async_computation.2 | async-start | bytes 786432 | tf_op jit(solution)/shard_map/psum | solution.py:12
  329.1 0.8 copy-start.9
  436.6 1.9 copy-start.17
  444.7 1.3 copy-start.12
  452.9 101.2 %all-reduce.17.cloned.1.call-start = ((), (), s32[]{:S(2)}) async-start(), calls=%async_computation.3 | async-start | bytes 3538944 | tf_op jit(solution)/shard_map/psum | solution.py:41
  489.3 2.8 copy-start.2
  554.1 2.2 copy-start.6
  557.4 0.8 copy-start.10
  570.0 0.6 copy-start.15
  585.7 0.7 copy-start.14
  674.5 1.9 copy-start.16
  680.6 1.3 copy-start.13
  686.4 1.3 copy-start.4
  687.2 2.5 copy-start.8
Sparse Core Ops, SparseCore 0:
  10.9 39.6 all-reduce.10
  55.7 59.5 all-reduce.20
  224.7 36.2 all-reduce.12
  266.1 59.5 all-reduce.18
  453.0 36.2 all-reduce.14
  494.5 59.5 all-reduce.16
where the time goes:
time: 701 us; the launch traced here: 697 us
  waiting for transfers between devices  292 us (42%)
  other arithmetic  285 us (41%)
  matrix products  53.1 us (8%)
  local copies, waits for them, and re-layouts  45.1 us (6%)
  between operations  20.7 us (3%)
    another operation x32, other arithmetic, shards(): factor = jnp.linalg.cholesky(gram_matrix)  182 us
    psum x3, waiting for transfers between devices, shards(): lax.psum((mult(panel_now.T, panel_now), mult(panel_now.T, working)), 'rows')  178 us
    psum x3, waiting for transfers between devices, spread(): return lax.psum(jnp.where(mine, shard, jnp.zeros_like(shard)), axis)  114 us
    another operation x4, other arithmetic, shards(): lax.linalg.triangular_solve(factor, identity, left_side=True, lower=True)  88.9 us
    dot_general x15, matrix products, mult(): jnp.dot(left, right, precision=lax.Precision.HIGHEST, preferred_element_t...  29.4 us
    another operation x31, local copies, waits for them, and re-layouts, shards(): lax.linalg.triangular_solve(factor, identity, left_side=True, lower=True)  23.1 us
  transfers between devices with their start and end apart: 6, of which 6 were waited for; matrix products, arithmetic and copies ran while one was open for 0% of the time, Pallas kernels for 0%

commit v1 on v0

--- a/solution.py
+++ b/solution.py
@@ -7,9 +7,15 @@
 PANELS = 3
 
 
+def gather_and_add(value, axis):
+    blocks = lax.all_gather(value, axis, axis=0, tiled=False)
+    total = blocks.sum(axis=0)
+    return total
+
+
 def spread(shard, axis, root):
     mine = lax.axis_index(axis) == root
-    return lax.psum(jnp.where(mine, shard, jnp.zeros_like(shard)), axis)
+    return gather_and_add(jnp.where(mine, shard, jnp.zeros_like(shard)), axis)
 
 
 def mult(left, right):

time: 701 us -> 671 us (0.957)
  other arithmetic: 285 us -> 275 us
  local copies, waits for them, and re-layouts: 45.1 us -> 36.2 us
  matrix products: 53.1 us -> 45 us
    psum x3 -> x0, waiting for transfers between devices: 114 us -> none  [spread(): return lax.psum(jnp.where(mine, shard, jnp.zeros_like(shard)), axis)]
    all_gather x0 -> x3, waiting for transfers between devices: none -> 114 us  [gather_and_add(): blocks = lax.all_gather(value, axis, axis=0, tiled=False)]
    another operation x32, other arithmetic: 182 us -> 171 us  [shards(): factor = jnp.linalg.cholesky(gram_matrix)]
where the time goes in v1:
time: 671 us; the launch traced here: 667 us
  waiting for transfers between devices  289 us (43%)
  other arithmetic  275 us (41%)
  matrix products  45 us (7%)
  local copies, waits for them, and re-layouts  36.2 us (5%)
  between operations  20.7 us (3%)
    psum x3, waiting for transfers between devices, shards(): lax.psum((mult(panel_now.T, panel_now), mult(panel_now.T, working)), 'rows')  176 us
    another operation x32, other arithmetic, shards(): factor = jnp.linalg.cholesky(gram_matrix)  171 us
    all_gather x3, waiting for transfers between devices, gather_and_add(): blocks = lax.all_gather(value, axis, axis=0, tiled=False)  114 us
    another operation x4, other arithmetic, shards(): lax.linalg.triangular_solve(factor, identity, left_side=True, lower=True)  88.9 us
    dot_general x15, matrix products, mult(): jnp.dot(left, right, precision=lax.Precision.HIGHEST, preferred_element_t...  27.7 us
    another operation x31, local copies, waits for them, and re-layouts, shards(): lax.linalg.triangular_solve(factor, identity, left_side=True, lower=True)  23.1 us
  transfers between devices with their start and end apart: 6, of which 6 were waited for; matrix products, arithmetic and copies ran while one was open for 0% of the time, Pallas kernels for 0%

profile of v1, /device:TPU:0, one launch (start us, length us, event | category | flops | bytes accessed | tf_op | source)
XLA Modules:
  0.0 667.4 jit_solution(10819419880143934225)
XLA Ops:
  7.2 1.8 slice_select_fusion
  9.1 40.8 %all-gather.7.cloned.1.call-done = f32[1024,384]{1,0:T(8,128)} async-done(((f32[256,384]{1,0:T(8,128)}), f32[1024,384]{1,0:T(8,128)}) %all-gather.7.cloned.1.call-update) | async-done | bytes 1572880 | tf_op jit(solution)/shard_map/all_gather | solution.py:11
  49.9 1.5 reduce_sum.27
  51.4 1.6 fusion.82
  53.1 2.1 fusion.83
  56.2 58.0 %all-reduce.12.cloned.1.call-done = (f32[384,384]{0,1:T(8,128)}, f32[384,768]{1,0:T(8,128)}) async-done(((f32[384,384]{0,1:T(8,128)}, f32[384,768]{1,0:T(8,128)}), (f32[384,384]{0,1:T(8,128)}, f32[384,768]{1,0:T(8,128)})) %all-reduce.12.cloned.1.call-update) | async-done | bytes 1769488 | tf_op jit(solution)/shard_map/psum | solution.py:47
  114.2 1.4 copy.4
  116.5 11.7 %cholesky.273 = f32[128,128]{1,0:T(8,128)S(1)} custom-call(f32[128,128]{1,0:T(8,128)S(1)} %cholesky.428), custom_call_target="Cholesky" | custom-call | tf_op jit(solution)/shard_map/jit(cholesky)/cholesky | solution.py:50
  128.3 9.8 %custom-call.23 = f32[1,128,128]{1,2,0:T(8,128)S(1)} custom-call(f32[1,128,128]{2,1,0:T(8,128)S(1)} %get-tuple-element.129), custom_call_target="InvertDiagBlocksLowerTriangular" | custom-call | tf_op jit(solution)/shard_map/jit(cholesky)/cholesky | solution.py:50
  139.3 1.2 convolution_subtract_fusion.11
  140.5 11.7 %cholesky.292 = f32[128,128]{1,0:T(8,128)S(1)} custom-call(f32[128,128]{1,0:T(8,128)S(1)} %cholesky.432), custom_call_target="Cholesky" | custom-call | tf_op jit(solution)/shard_map/jit(cholesky)/cholesky | solution.py:50
  152.2 10.0 %custom-call.24 = f32[1,128,128]{1,2,0:T(8,128)S(1)} custom-call(f32[1,128,128]{2,1,0:T(8,128)S(1)} %get-tuple-element.126), custom_call_target="InvertDiagBlocksLowerTriangular" | custom-call | tf_op jit(solution)/shard_map/jit(cholesky)/cholesky | solution.py:50
  163.5 11.7 %cholesky.311 = f32[128,128]{1,0:T(8,128)S(1)} custom-call(f32[128,128]{1,0:T(8,128)S(1)} %convolution_subtract_fusion.14), custom_call_target="Cholesky" | custom-call | tf_op jit(solution)/shard_map/jit(cholesky)/cholesky | solution.py:50
  179.4 8.7 %while.9 = (s32[]{:T(128)}, f32[384,384]{1,0:T(8,128)}, s32[3,2]{0,1:T(2,128)S(1)}, f32[3,128,128]{2,1,0:T(8,128)S(1)}, s32[]{:T(128)}) while((s32[]{:T(128)}, f32[384,384]{1,0:T(8,128)}, s32[3,2]{0,1:T(2,128)S(1)}, f32[3,128,128]{2,1,0:T(8,128)S(1)}, s32[]{:T(128)}) %tuple.93), condition=%wide.while_cond.3, body=%wide.while_body.3.sunk | while | flops 2 | bytes 131189 | solution.py:51
  180.1 2.3 bitcast_dynamic-update-slice_fusion.6
  183.0 2.3 bitcast_dynamic-update-slice_fusion.6
  185.9 2.2 bitcast_dynamic-update-slice_fusion.6
  188.1 29.9 %custom-call.25 = f32[3,128,128]{1,2,0:T(8,128)S(1)} custom-call(f32[3,128,128]{2,1,0:T(8,128)S(1)} %get-tuple-element.60), custom_call_target="InvertDiagBlocksLowerTriangular" | custom-call | tf_op jit(solution)/shard_map/triangular_solve/custom-call.2 | solution.py:51
  219.9 1.3 convolution_subtract_fusion.7
  221.6 1.7 fusion.13
  225.2 3.1 add_multiply_fusion.2
  228.4 1.4 convolution_subtract_fusion.2
  229.8 1.4 broadcast_select_fusion.1
  231.3 36.4 %all-gather.9.cloned.1.call-done = f32[1024,384]{1,0:T(8,128)} async-done(((f32[256,384]{1,0:T(8,128)}), f32[1024,384]{1,0:T(8,128)}) %all-gather.9.cloned.1.call-update) | async-done | bytes 1572880 | tf_op jit(solution)/shard_map/all_gather | solution.py:11
  267.8 1.5 reduce_sum.28
  269.3 1.6 fusion.84
  270.9 2.2 fusion.85
  273.4 58.7 %all-reduce.10.cloned.1.call-done = (f32[384,384]{0,1:T(8,128)}, f32[384,768]{1,0:T(8,128)}) async-done(((f32[384,384]{0,1:T(8,128)}, f32[384,768]{1,0:T(8,128)}), (f32[384,384]{0,1:T(8,128)}, f32[384,768]{1,0:T(8,128)})) %all-reduce.10.cloned.1.call-update) | async-done | bytes 1769488 | tf_op jit(solution)/shard_map/psum | solution.py:47
  332.1 1.4 copy.6
  333.6 11.7 %cholesky.326 = f32[128,128]{1,0:T(8,128)S(1)} custom-call(f32[128,128]{1,0:T(8,128)S(1)} %cholesky.436), custom_call_target="Cholesky" | custom-call | tf_op jit(solution)/shard_map/jit(cholesky)/cholesky | solution.py:50
  345.4 9.8 %custom-call.26 = f32[1,128,128]{1,2,0:T(8,128)S(1)} custom-call(f32[1,128,128]{2,1,0:T(8,128)S(1)} %get-tuple-element.122), custom_call_target="InvertDiagBlocksLowerTriangular" | custom-call | tf_op jit(solution)/shard_map/jit(cholesky)/cholesky | solution.py:50
  355.7 11.7 %cholesky.345 = f32[128,128]{1,0:T(8,128)S(1)} custom-call(f32[128,128]{1,0:T(8,128)S(1)} %cholesky.440), custom_call_target="Cholesky" | custom-call | tf_op jit(solution)/shard_map/jit(cholesky)/cholesky | solution.py:50
  367.5 10.2 %custom-call.27 = f32[1,128,128]{1,2,0:T(8,128)S(1)} custom-call(f32[1,128,128]{2,1,0:T(8,128)S(1)} %get-tuple-element.119), custom_call_target="InvertDiagBlocksLowerTriangular" | custom-call | tf_op jit(solution)/shard_map/jit(cholesky)/cholesky | solution.py:50
  378.2 11.7 %cholesky.364 = f32[128,128]{1,0:T(8,128)S(1)} custom-call(f32[128,128]{1,0:T(8,128)S(1)} %convolution_subtract_fusion.13), custom_call_target="Cholesky" | custom-call | tf_op jit(solution)/shard_map/jit(cholesky)/cholesky | solution.py:50
  394.6 5.8 while.10
  395.2 1.3 bitcast_dynamic-update-slice_fusion.7
  397.2 1.3 bitcast_dynamic-update-slice_fusion.7
  399.1 1.3 bitcast_dynamic-update-slice_fusion.7
  400.4 29.5 %custom-call.28 = f32[3,128,128]{1,2,0:T(8,128)S(1)} custom-call(f32[3,128,128]{2,1,0:T(8,128)S(1)} %get-tuple-element.61), custom_call_target="InvertDiagBlocksLowerTriangular" | custom-call | tf_op jit(solution)/shard_map/triangular_solve/custom-call.2 | solution.py:51
  432.7 1.3 copy.10
  435.7 3.1 add_multiply_fusion.1
  438.8 1.4 convolution_subtract_fusion.1
  440.3 1.4 broadcast_select_fusion
  441.9 36.2 %all-gather.11.cloned.1.call-done = f32[1024,384]{1,0:T(8,128)} async-done(((f32[256,384]{1,0:T(8,128)}), f32[1024,384]{1,0:T(8,128)}) %all-gather.11.cloned.1.call-update) | async-done | bytes 1572880 | tf_op jit(solution)/shard_map/all_gather | solution.py:11
  478.2 1.5 reduce_sum.29
  479.7 1.6 fusion.86
  481.4 2.2 fusion.87
  483.6 58.9 %all-reduce.8.cloned.1.call-done = (f32[384,384]{0,1:T(8,128)}, f32[384,768]{1,0:T(8,128)}) async-done(((f32[384,384]{0,1:T(8,128)}, f32[384,768]{1,0:T(8,128)}), (f32[384,384]{0,1:T(8,128)}, f32[384,768]{1,0:T(8,128)})) %all-reduce.8.cloned.1.call-update) | async-done | bytes 1769488 | tf_op jit(solution)/shard_map/psum | solution.py:47
  542.5 1.4 copy.8
  544.7 11.7 %cholesky.379 = f32[128,128]{1,0:T(8,128)S(1)} custom-call(f32[128,128]{1,0:T(8,128)S(1)} %cholesky.444), custom_call_target="Cholesky" | custom-call | tf_op jit(solution)/shard_map/jit(cholesky)/cholesky | solution.py:50
  556.5 9.8 %custom-call.29 = f32[1,128,128]{1,2,0:T(8,128)S(1)} custom-call(f32[1,128,128]{2,1,0:T(8,128)S(1)} %get-tuple-element.115), custom_call_target="InvertDiagBlocksLowerTriangular" | custom-call | tf_op jit(solution)/shard_map/jit(cholesky)/cholesky | solution.py:50
  567.5 1.2 convolution_subtract_fusion.9
  568.7 11.9 %cholesky.398 = f32[128,128]{1,0:T(8,128)S(1)} custom-call(f32[128,128]{1,0:T(8,128)S(1)} %cholesky.448), custom_call_target="Cholesky" | custom-call | tf_op jit(solution)/shard_map/jit(cholesky)/cholesky | solution.py:50
  580.7 9.8 %custom-call.30 = f32[1,128,128]{1,2,0:T(8,128)S(1)} custom-call(f32[1,128,128]{2,1,0:T(8,128)S(1)} %get-tuple-element.112), custom_call_target="InvertDiagBlocksLowerTriangular" | custom-call | tf_op jit(solution)/shard_map/jit(cholesky)/cholesky | solution.py:50
  591.8 11.7 %cholesky.417 = f32[128,128]{1,0:T(8,128)S(1)} custom-call(f32[128,128]{1,0:T(8,128)S(1)} %convolution_subtract_fusion.12), custom_call_target="Cholesky" | custom-call | tf_op jit(solution)/shard_map/jit(cholesky)/cholesky | solution.py:50
  608.4 9.0 %while.11 = (s32[]{:T(128)}, f32[384,384]{1,0:T(8,128)}, s32[3,2]{0,1:T(2,128)S(1)}, f32[3,128,128]{2,1,0:T(8,128)S(1)}, s32[]{:T(128)}) while((s32[]{:T(128)}, f32[384,384]{1,0:T(8,128)}, s32[3,2]{0,1:T(2,128)S(1)}, f32[3,128,128]{2,1,0:T(8,128)S(1)}, s32[]{:T(128)}) %tuple.118), condition=%wide.while_cond.3.clone.1, body=%wide.while_body.3.clone.1.sunk | while | flops 2 | bytes 131189 | solution.py:51
  609.3 2.2 bitcast_dynamic-update-slice_fusion.8
  612.2 2.2 bitcast_dynamic-update-slice_fusion.8
  615.2 2.2 bitcast_dynamic-update-slice_fusion.8
  617.4 29.5 %custom-call.31 = f32[3,128,128]{1,2,0:T(8,128)S(1)} custom-call(f32[3,128,128]{2,1,0:T(8,128)S(1)} %get-tuple-element.62), custom_call_target="InvertDiagBlocksLowerTriangular" | custom-call | tf_op jit(solution)/shard_map/triangular_solve/custom-call.2 | solution.py:51
  648.8 1.3 convolution_subtract_fusion.3
  653.3 2.1 add_multiply_fusion
  655.5 1.5 convolution_subtract_fusion
  658.2 2.0 pad_maximum_fusion
  (132 shorter events, 38.4 us)
Async XLA Ops:
  7.2 42.7 %all-gather.7.cloned.1.call-start = ((), (), s32[]{:S(2)}) async-start(), calls=%async_computation | async-start | bytes 1966080 | tf_op jit(solution)/shard_map/all_gather | solution.py:11
  9.0 105.2 %all-reduce.12.cloned.1.call-start = ((), (), s32[]{:S(2)}) async-start(), calls=%async_computation.5 | async-start | bytes 3538944 | tf_op jit(solution)/shard_map/psum | solution.py:47
  51.4 1.7 copy-start
  55.3 212.5 %all-gather.9.cloned.1.call-start = ((), (), s32[]{:S(2)}) async-start(), calls=%async_computation.1 | async-start | bytes 1966080 | tf_op jit(solution)/shard_map/all_gather | solution.py:11
  114.2 1.4 copy-start.4
  115.7 0.8 copy-start.8
  223.9 1.3 copy-start.10
  225.2 3.1 copy-start.3
  231.3 100.8 %all-reduce.10.cloned.1.call-start = ((), (), s32[]{:S(2)}) async-start(), calls=%async_computation.4 | async-start | bytes 3538944 | tf_op jit(solution)/shard_map/psum | solution.py:47
  273.2 205.0 %all-gather.11.cloned.1.call-start = ((), (), s32[]{:S(2)}) async-start(), calls=%async_computation.2 | async-start | bytes 1966080 | tf_op jit(solution)/shard_map/all_gather | solution.py:11
  332.1 1.4 copy-start.5
  434.4 1.3 copy-start.11
  441.7 100.8 %all-reduce.8.cloned.1.call-start = ((), (), s32[]{:S(2)}) async-start(), calls=%async_computation.3 | async-start | bytes 3538944 | tf_op jit(solution)/shard_map/psum | solution.py:47
  542.5 1.4 copy-start.6
  543.9 0.8 copy-start.9
  652.0 1.3 copy-start.12
  655.5 2.3 copy-start.2
  656.9 1.3 copy-start.1
  657.7 2.5 copy-start.7
Sparse Core Ops, SparseCore 0:
  10.1 39.7 all-gather.6
  55.4 58.7 all-reduce.11
  231.4 36.3 all-gather.8
  273.3 58.7 all-reduce.9
  441.8 36.3 all-gather.10
  483.7 58.7 all-reduce.7
